TPU v7x, 256 devices: a whole 4x4x8 slice. The times are simulated.
256 devices in a mesh: panel: 16 (over z, core), tm: 16 (over x, y).
Axes of the slice: x: 4, y: 4, z: 8, core: 2. Of those that a mesh axis runs over, the one named last changes fastest.
Arguments:
- pressures: bfloat16 [98304, 12288], P('panel', 'tm'), may hold values from -60 to 60
- sketch: bfloat16 [98304, 128], P(('panel', 'tm')), may hold values from -6 to 6
Outputs:
- basis_rows: bfloat16 [12288, 128], P('tm')
- image: float32 [98304, 128], P(('panel', 'tm'))
All inputs are finite; a program needn't handle non-finite values.
Results may differ from a plain program's by a relative error of at most 0.0029.
Values may be sent and summed in bfloat16 or wider, within the bound.
No kernel may reach another device: no remote copies, remote signals or barrier semaphores. Data moves between devices by JAX's collectives and lax.ppermute only.
A program may use at most 64 MiB of HBM per device.

v0:
```python
import jax
import jax.numpy as jnp
from jax import lax
from jax.sharding import PartitionSpec as P


def gram_of(rows_block):
    return lax.dot_general(
        rows_block,
        rows_block,
        (((0,), (0,)), ((), ())),
        precision=lax.Precision.HIGHEST,
        preferred_element_type=jnp.float32,
    )


def orthonormal(rows_block, gram_matrix):
    lower_factor = jnp.linalg.cholesky(gram_matrix)
    solved = jax.scipy.linalg.solve_triangular(lower_factor, rows_block.T, lower=True)
    return solved.T.astype(jnp.bfloat16)


def on_device(pressures, sketch):
    partial_y = lax.dot_general(
        pressures,
        lax.all_gather(sketch, "tm", axis=0, tiled=True),
        (((0,), (0,)), ((), ())),
        preferred_element_type=jnp.float32,
    )
    y_rows = lax.psum(partial_y, "panel")
    gram_matrix = lax.psum(gram_of(y_rows), "tm")
    basis_rows = orthonormal(y_rows, gram_matrix)
    own_rows = pressures.shape[0] // lax.axis_size("tm")
    full_image = lax.psum(jnp.dot(pressures, basis_rows, preferred_element_type=jnp.float32), "tm")
    image = lax.dynamic_slice_in_dim(full_image, lax.axis_index("tm") * own_rows, own_rows, 0)
    return (basis_rows, image)


def solution(mesh):
    return jax.shard_map(
        on_device,
        mesh=mesh,
        in_specs=(P("panel", "tm"), P(("panel", "tm"), None)),
        out_specs=(P("tm", None), P(("panel", "tm"), None)),
        check_vma=False,
    )
```

profile of v0, /device:TPU:1, one launch (start us, length us, event | category | flops | bytes accessed | tf_op | source)
XLA Modules:
  0.0 423.2 jit_solution(15949933175070414837)
XLA Ops:
  7.2 0.0 all-gather.2.cloned.1.call-start
  7.2 0.7 all-gather.2.cloned.1.call-update
  7.9 0.0 all-reduce.4.cloned.1.call-start
  7.9 54.4 %all-gather.2.cloned.1.call-done = bf16[6144,128]{1,0:T(8,128)(2,1)} async-done(((bf16[384,128]{1,0:T(8,128)(2,1)}), bf16[6144,128]{1,0:T(8,128)(2,1)}) %all-gather.2.cloned.1.call-update) | async-done | bytes 1572880 | tf_op jit(solution)/shard_map/all_gather | solution.py:26
  62.3 7.5 %fusion.3 = f32[768,128]{1,0:T(8,128)} fusion(bf16[6144,768]{1,0:T(8,128)(2,1)} %param.2, bf16[6144,128]{1,0:T(8,128)(2,1)} %all-gather.2.cloned.1.call-done), kind=kOutput, calls=%fused_computation.12 | convolution fusion | flops 1207959552 | bytes 11403264 | tf_op jit(solution)/shard_map/dot_general | solution.py:24
  69.8 0.0 all-reduce.4.cloned.1.call-update
  69.8 0.0 all-reduce.6.cloned.1.call-start
  69.9 109.7 %all-reduce.4.cloned.1.call-done = f32[768,128]{1,0:T(8,128)} async-done(((f32[768,128]{1,0:T(8,128)}), f32[768,128]{1,0:T(8,128)}) %all-reduce.4.cloned.1.call-update) | async-done | bytes 393232 | tf_op jit(solution)/shard_map/psum | solution.py:30
  179.6 2.5 fusion.4
  182.1 0.0 all-reduce.6.cloned.1.call-update
  182.2 0.2 all-reduce.8.cloned.1.call-start
  182.4 91.2 %all-reduce.6.cloned.1.call-done = f32[128,128]{0,1:T(8,128)} async-done(((f32[128,128]{0,1:T(8,128)}), f32[128,128]{0,1:T(8,128)}) %all-reduce.6.cloned.1.call-update) | async-done | bytes 65552 | tf_op jit(solution)/shard_map/psum | solution.py:31
  273.5 0.9 copy.5
  274.5 0.9 fusion.2
  275.3 11.7 %cholesky.16 = f32[128,128]{1,0:T(8,128)S(1)} custom-call(f32[128,128]{1,0:T(8,128)S(1)} %fusion.2), custom_call_target="Cholesky" | custom-call | tf_op jit(solution)/shard_map/jit(cholesky)/cholesky | solution.py:18
  287.1 0.6 compare_reduce_fusion
  287.7 0.7 fusion
  288.4 9.8 %custom-call.7 = f32[1,128,128]{1,2,0:T(8,128)S(1)} custom-call(f32[1,128,128]{2,1,0:T(8,128)S(1)} %fusion), custom_call_target="InvertDiagBlocksLowerTriangular" | custom-call | tf_op jit(solution)/shard_map/jit(_solve_triangular)/triangular_solve | solution.py:19
  298.2 1.5 convolution_convert_fusion
  299.7 0.0 copy-start
  299.7 8.7 %convolution_bitcast_fusion = f32[6144,128]{0,1:T(8,128)} fusion(bf16[768,128]{1,0:T(8,128)(2,1)S(1)} %convolution_convert_fusion, bf16[6144,768]{1,0:T(8,128)(2,1)} %param.2), kind=kOutput, calls=%fused_computation | convolution fusion | flops 1207959552 | bytes 12779520 | tf_op jit(solution)/shard_map/dot_general | solution.py:34
  308.3 0.0 copy-done
  308.3 0.0 all-reduce.8.cloned.1.call-update
  308.4 106.5 %all-reduce.8.cloned.1.call-done = f32[6144,128]{0,1:T(8,128)} async-done(((f32[6144,128]{0,1:T(8,128)}), f32[6144,128]{0,1:T(8,128)}) %all-reduce.8.cloned.1.call-update) | async-done | bytes 3145744 | tf_op jit(solution)/shard_map/psum | solution.py:34
  414.9 0.9 constant_dynamic-slice_fusion
  415.8 0.8 copy.6
  (1 shorter events, 0.0 us)
Async XLA Ops:
  7.2 55.2 %all-gather.2.cloned.1.call-start = ((), (), s32[]{:S(2)}) async-start(), calls=%async_computation | async-start | bytes 1671168 | tf_op jit(solution)/shard_map/all_gather | solution.py:26
  7.9 171.7 %all-reduce.4.cloned.1.call-start = ((), (), s32[]{:S(2)}) async-start(), calls=%async_computation.1 | async-start | bytes 786432 | tf_op jit(solution)/shard_map/psum | solution.py:30
  69.8 203.7 %all-reduce.6.cloned.1.call-start = ((), (), s32[]{:S(2)}) async-start(), calls=%async_computation.2 | async-start | bytes 131072 | tf_op jit(solution)/shard_map/psum | solution.py:31
  182.2 232.8 %all-reduce.8.cloned.1.call-start = ((), (), s32[]{:S(2)}) async-start(), calls=%async_computation.3 | async-start | bytes 6291456 | tf_op jit(solution)/shard_map/psum | solution.py:34
  299.7 8.7 %copy-start = (bf16[768,128]{1,0:T(8,128)(2,1)}, bf16[768,128]{1,0:T(8,128)(2,1)S(1)}, u32[]{:S(2)}) copy-start(bf16[768,128]{1,0:T(8,128)(2,1)S(1)} %convolution_convert_fusion) | copy-start | bytes 589828
Sparse Core Ops, SparseCore 0:
  10.5 51.7 all-gather.1
  69.9 109.6 all-reduce.3
  183.7 89.8 all-reduce.5
  308.5 106.3 all-reduce.7
where the time goes:
time: 424 us; the launch traced here: 423 us
  waiting for transfers between devices  363 us (86%)
  other arithmetic  23.7 us (6%)
  matrix products  20.1 us (5%)
  between operations  13.8 us (3%)
    psum x1, waiting for transfers between devices, on_device(): y_rows = lax.psum(partial_y, 'panel')  110 us
    psum x1, waiting for transfers between devices, on_device(): lax.psum(jnp.dot(pressures, basis_rows, preferred_element_type=jnp.float3...  107 us
    psum x1, waiting for transfers between devices, on_device(): gram_matrix = lax.psum(gram_of(y_rows), 'tm')  91.2 us
    all_gather x1, waiting for transfers between devices, on_device(): lax.all_gather(sketch, 'tm', axis=0, tiled=True)  54.4 us
    another operation x3, other arithmetic, orthonormal(): lower_factor = jnp.linalg.cholesky(gram_matrix)  12.4 us
    another operation x2, other arithmetic, orthonormal(): jax.scipy.linalg.solve_triangular(lower_factor, rows_block.T, lower=True)  10.5 us
    dot_general x1, matrix products, on_device(): jnp.dot(pressures, basis_rows, preferred_element_type=jnp.float32)  8.66 us
  transfers between devices with their start and end apart: 4, of which 4 were waited for; matrix products, arithmetic and copies ran while one was open for 0% of the time, Pallas kernels for 0%

commit v1 on v0

--- a/solution.py
+++ b/solution.py
@@ -23,7 +23,9 @@
 def on_device(pressures, sketch):
     partial_y = lax.dot_general(
         pressures,
-        lax.all_gather(sketch, "tm", axis=0, tiled=True),
+        jnp.concatenate(
+            lax.all_to_all(jnp.stack([sketch] * lax.axis_size("tm")), "tm", 0, 0), axis=0
+        ),
         (((0,), (0,)), ((), ())),
         preferred_element_type=jnp.float32,
     )

time: 424 us -> 399 us (0.941)
  waiting for transfers between devices: 363 us -> 308 us
  blocking collectives: 0 us -> 28.9 us
    all_gather x1 -> x0, waiting for transfers between devices: 54.4 us -> none  [on_device(): lax.all_gather(sketch, 'tm', axis=0, tiled=True)]
    all_to_all x0 -> x1, blocking collectives: none -> 28.9 us  [on_device(): lax.all_to_all(jnp.stack([sketch] * lax.axis_size('tm')), 'tm', 0, 0)]
  transfers between devices with their start and end apart: 4 -> 3, of which waited for: 4 -> 3; matrix products, arithmetic and copies ran while one was open for 0% -> 0% of each run, Pallas kernels for 0% -> 0%
where the time goes in v1:
time: 399 us; the launch traced here: 398 us
  waiting for transfers between devices  308 us (77%)
  blocking collectives  28.9 us (7%)
  other arithmetic  23.7 us (6%)
  matrix products  19.7 us (5%)
  between operations  13.8 us (3%)
    psum x1, waiting for transfers between devices, on_device(): y_rows = lax.psum(partial_y, 'panel')  110 us
    psum x1, waiting for transfers between devices, on_device(): lax.psum(jnp.dot(pressures, basis_rows, preferred_element_type=jnp.float3...  107 us
    psum x1, waiting for transfers between devices, on_device(): gram_matrix = lax.psum(gram_of(y_rows), 'tm')  91.1 us
    all_to_all x1, blocking collectives, on_device(): lax.all_to_all(jnp.stack([sketch] * lax.axis_size('tm')), 'tm', 0, 0)  28.9 us
    another operation x3, other arithmetic, orthonormal(): lower_factor = jnp.linalg.cholesky(gram_matrix)  12.4 us
    another operation x2, other arithmetic, orthonormal(): jax.scipy.linalg.solve_triangular(lower_factor, rows_block.T, lower=True)  10.5 us
    dot_general x1, matrix products, on_device(): jnp.dot(pressures, basis_rows, preferred_element_type=jnp.float32)  8.66 us
  transfers between devices with their start and end apart: 3, of which 3 were waited for; matrix products, arithmetic and copies ran while one was open for 0% of the time, Pallas kernels for 0%

profile of v1, /device:TPU:1, one launch (start us, length us, event | category | flops | bytes accessed | tf_op | source)
XLA Modules:
  0.0 398.5 jit_solution(15951695205928496795)
XLA Ops:
  7.2 0.0 all-reduce.4.cloned.1.call-start
  7.2 1.2 stack.2
  8.4 28.9 %all_to_all.5 = bf16[16,384,128]{2,1,0:T(8,128)(2,1)S(1)} all-to-all(bf16[16,384,128]{2,1,0:T(8,128)(2,1)S(1)} %stack.2), channel_id=1, replica_groups=mesh['panel'=16,'tm'=16] {'tm'}, dimensions={0} | all-to-all | bytes 3145728 | tf_op jit(solution)/shard_map/all_to_all | solution.py:27
  37.3 7.1 %fusion.3 = f32[768,128]{1,0:T(8,128)} fusion(bf16[6144,768]{1,0:T(8,128)(2,1)} %param.2, bf16[6144,128]{1,0:T(8,128)(2,1)S(1)} %bitcast.19), kind=kOutput, calls=%fused_computation.12 | convolution fusion | flops 1207959552 | bytes 11403264 | tf_op jit(solution)/shard_map/dot_general | solution.py:24
  44.4 0.0 all-reduce.4.cloned.1.call-update
  44.4 0.0 all-reduce.6.cloned.1.call-start
  44.4 110.5 %all-reduce.4.cloned.1.call-done = f32[768,128]{1,0:T(8,128)} async-done(((f32[768,128]{1,0:T(8,128)}), f32[768,128]{1,0:T(8,128)}) %all-reduce.4.cloned.1.call-update) | async-done | bytes 393232 | tf_op jit(solution)/shard_map/psum | solution.py:32
  154.9 2.5 fusion.4
  157.4 0.0 all-reduce.6.cloned.1.call-update
  157.5 0.2 all-reduce.8.cloned.1.call-start
  157.7 91.1 %all-reduce.6.cloned.1.call-done = f32[128,128]{0,1:T(8,128)} async-done(((f32[128,128]{0,1:T(8,128)}), f32[128,128]{0,1:T(8,128)}) %all-reduce.6.cloned.1.call-update) | async-done | bytes 65552 | tf_op jit(solution)/shard_map/psum | solution.py:33
  248.8 0.9 copy.5
  249.8 0.9 fusion.2
  250.6 11.7 %cholesky.16 = f32[128,128]{1,0:T(8,128)S(1)} custom-call(f32[128,128]{1,0:T(8,128)S(1)} %fusion.2), custom_call_target="Cholesky" | custom-call | tf_op jit(solution)/shard_map/jit(cholesky)/cholesky | solution.py:18
  262.4 0.6 compare_reduce_fusion
  263.0 0.7 fusion
  263.7 9.8 %custom-call.7 = f32[1,128,128]{1,2,0:T(8,128)S(1)} custom-call(f32[1,128,128]{2,1,0:T(8,128)S(1)} %fusion), custom_call_target="InvertDiagBlocksLowerTriangular" | custom-call | tf_op jit(solution)/shard_map/jit(_solve_triangular)/triangular_solve | solution.py:19
  273.5 1.5 convolution_convert_fusion
  275.0 0.0 copy-start
  275.0 8.7 %convolution_bitcast_fusion = f32[6144,128]{0,1:T(8,128)} fusion(bf16[768,128]{1,0:T(8,128)(2,1)S(1)} %convolution_convert_fusion, bf16[6144,768]{1,0:T(8,128)(2,1)} %param.2), kind=kOutput, calls=%fused_computation | convolution fusion | flops 1207959552 | bytes 12779520 | tf_op jit(solution)/shard_map/dot_general | solution.py:36
  283.6 0.0 copy-done
  283.6 0.0 all-reduce.8.cloned.1.call-update
  283.7 106.5 %all-reduce.8.cloned.1.call-done = f32[6144,128]{0,1:T(8,128)} async-done(((f32[6144,128]{0,1:T(8,128)}), f32[6144,128]{0,1:T(8,128)}) %all-reduce.8.cloned.1.call-update) | async-done | bytes 3145744 | tf_op jit(solution)/shard_map/psum | solution.py:36
  390.2 0.9 constant_dynamic-slice_fusion
  391.2 0.8 copy.6
  (1 shorter events, 0.0 us)
Async XLA Ops:
  7.2 147.7 %all-reduce.4.cloned.1.call-start = ((), (), s32[]{:S(2)}) async-start(), calls=%async_computation.1 | async-start | bytes 786432 | tf_op jit(solution)/shard_map/psum | solution.py:32
  44.4 204.5 %all-reduce.6.cloned.1.call-start = ((), (), s32[]{:S(2)}) async-start(), calls=%async_computation.2 | async-start | bytes 131072 | tf_op jit(solution)/shard_map/psum | solution.py:33
  157.5 232.7 %all-reduce.8.cloned.1.call-start = ((), (), s32[]{:S(2)}) async-start(), calls=%async_computation.3 | async-start | bytes 6291456 | tf_op jit(solution)/shard_map/psum | solution.py:36
  275.0 8.7 %copy-start = (bf16[768,128]{1,0:T(8,128)(2,1)}, bf16[768,128]{1,0:T(8,128)(2,1)S(1)}, u32[]{:S(2)}) copy-start(bf16[768,128]{1,0:T(8,128)(2,1)S(1)} %convolution_convert_fusion) | copy-start | bytes 589828
Sparse Core Ops, SparseCore 0:
  44.5 110.3 all-reduce.3
  159.0 89.8 all-reduce.5
  283.8 106.3 all-reduce.7

commit v2 on v0

--- a/solution.py
+++ b/solution.py
@@ -28,7 +28,7 @@
         preferred_element_type=jnp.float32,
     )
     y_rows = lax.psum(partial_y, "panel")
-    gram_matrix = lax.psum(gram_of(y_rows), "tm")
+    gram_matrix = jnp.sum(lax.all_gather(gram_of(y_rows), "tm"), axis=0)
     basis_rows = orthonormal(y_rows, gram_matrix)
     own_rows = pressures.shape[0] // lax.axis_size("tm")
     full_image = lax.psum(jnp.dot(pressures, basis_rows, preferred_element_type=jnp.float32), "tm")

time: 424 us -> 379 us (0.89)
  waiting for transfers between devices: 363 us -> 318 us
    psum x1 -> x0, waiting for transfers between devices: 91.2 us -> none  [on_device(): gram_matrix = lax.psum(gram_of(y_rows), 'tm')]
    all_gather x0 -> x1, waiting for transfers between devices: none -> 47.2 us  [on_device(): gram_matrix = jnp.sum(lax.all_gather(gram_of(y_rows), 'tm'), axis=0)]
where the time goes in v2:
time: 379 us
  waiting for transfers between devices  318 us (84%)
  other arithmetic  24.1 us (6%)
  matrix products  20.1 us (5%)
  between operations  13.8 us (4%)
    psum x1, waiting for transfers between devices, on_device(): y_rows = lax.psum(partial_y, 'panel')  110 us
    psum x1, waiting for transfers between devices, on_device(): lax.psum(jnp.dot(pressures, basis_rows, preferred_element_type=jnp.float3...  106 us
    all_gather x1, waiting for transfers between devices, on_device(): lax.all_gather(sketch, 'tm', axis=0, tiled=True)  54.4 us
    all_gather x1, waiting for transfers between devices, on_device(): gram_matrix = jnp.sum(lax.all_gather(gram_of(y_rows), 'tm'), axis=0)  47.2 us
    another operation x3, other arithmetic, orthonormal(): lower_factor = jnp.linalg.cholesky(gram_matrix)  12.4 us
    another operation x2, other arithmetic, orthonormal(): jax.scipy.linalg.solve_triangular(lower_factor, rows_block.T, lower=True)  10.5 us
    dot_general x1, matrix products, on_device(): jnp.dot(pressures, basis_rows, preferred_element_type=jnp.float32)  8.65 us
  transfers between devices with their start and end apart: 4, of which 4 were waited for; matrix products, arithmetic and copies ran while one was open for 0% of the time, Pallas kernels for 0%

profile of v2, /device:TPU:1, one launch (start us, length us, event | category | flops | bytes accessed | tf_op | source)
XLA Modules:
  0.0 378.6 jit_solution(1641575515055281031)
XLA Ops:
  7.2 0.0 all-gather.4.cloned.1.call-start
  7.2 0.7 all-gather.4.cloned.1.call-update
  7.9 0.0 all-reduce.3.cloned.1.call-start
  7.9 54.4 %all-gather.4.cloned.1.call-done = bf16[6144,128]{1,0:T(8,128)(2,1)} async-done(((bf16[384,128]{1,0:T(8,128)(2,1)}), bf16[6144,128]{1,0:T(8,128)(2,1)}) %all-gather.4.cloned.1.call-update) | async-done | bytes 1572880 | tf_op jit(solution)/shard_map/all_gather | solution.py:26
  62.3 7.5 %fusion.3 = f32[768,128]{1,0:T(8,128)} fusion(bf16[6144,768]{1,0:T(8,128)(2,1)} %param.2, bf16[6144,128]{1,0:T(8,128)(2,1)} %all-gather.4.cloned.1.call-done), kind=kOutput, calls=%fused_computation.12 | convolution fusion | flops 1207959552 | bytes 11403264 | tf_op jit(solution)/shard_map/dot_general | solution.py:24
  69.8 0.0 all-reduce.3.cloned.1.call-update
  69.8 0.0 all-gather.6.cloned.1.call-start
  69.9 109.7 %all-reduce.3.cloned.1.call-done = f32[768,128]{1,0:T(8,128)} async-done(((f32[768,128]{1,0:T(8,128)}), f32[768,128]{1,0:T(8,128)}) %all-reduce.3.cloned.1.call-update) | async-done | bytes 393232 | tf_op jit(solution)/shard_map/psum | solution.py:30
  179.6 2.5 fusion.4
  182.1 0.0 all-gather.6.cloned.1.call-update
  182.2 0.2 all-reduce.5.cloned.1.call-start
  182.4 47.2 %all-gather.6.cloned.1.call-done = f32[2048,128]{1,0:T(8,128)} async-done(((f32[128,128]{1,0:T(8,128)}), f32[2048,128]{1,0:T(8,128)}) %all-gather.6.cloned.1.call-update) | async-done | bytes 1048592 | tf_op jit(solution)/shard_map/all_gather | solution.py:31
  229.6 1.3 reduce_sum.9
  230.9 0.1 copy.6
  231.0 11.7 %cholesky.16 = f32[128,128]{1,0:T(8,128)S(1)} custom-call(f32[128,128]{1,0:T(8,128)S(1)} %fusion.2), custom_call_target="Cholesky" | custom-call | tf_op jit(solution)/shard_map/jit(cholesky)/cholesky | solution.py:18
  242.7 0.6 compare_reduce_fusion
  243.4 0.7 fusion
  244.0 9.8 %custom-call.7 = f32[1,128,128]{1,2,0:T(8,128)S(1)} custom-call(f32[1,128,128]{2,1,0:T(8,128)S(1)} %fusion), custom_call_target="InvertDiagBlocksLowerTriangular" | custom-call | tf_op jit(solution)/shard_map/jit(_solve_triangular)/triangular_solve | solution.py:19
  253.9 1.5 convolution_convert_fusion
  255.3 0.0 copy-start
  255.3 8.7 %convolution_bitcast_fusion = f32[6144,128]{0,1:T(8,128)} fusion(bf16[768,128]{1,0:T(8,128)(2,1)S(1)} %convolution_convert_fusion, bf16[6144,768]{1,0:T(8,128)(2,1)} %param.2), kind=kOutput, calls=%fused_computation | convolution fusion | flops 1207959552 | bytes 12779520 | tf_op jit(solution)/shard_map/dot_general | solution.py:34
  264.0 0.0 copy-done
  264.0 0.0 all-reduce.5.cloned.1.call-update
  264.0 106.3 %all-reduce.5.cloned.1.call-done = f32[6144,128]{0,1:T(8,128)} async-done(((f32[6144,128]{0,1:T(8,128)}), f32[6144,128]{0,1:T(8,128)}) %all-reduce.5.cloned.1.call-update) | async-done | bytes 3145744 | tf_op jit(solution)/shard_map/psum | solution.py:34
  370.3 0.9 constant_dynamic-slice_fusion
  371.3 0.8 copy.7
  (2 shorter events, 0.0 us)
Async XLA Ops:
  7.2 55.2 %all-gather.4.cloned.1.call-start = ((), (), s32[]{:S(2)}) async-start(), calls=%async_computation | async-start | bytes 1671168 | tf_op jit(solution)/shard_map/all_gather | solution.py:26
  7.9 171.7 %all-reduce.3.cloned.1.call-start = ((), (), s32[]{:S(2)}) async-start(), calls=%async_computation.1 | async-start | bytes 786432 | tf_op jit(solution)/shard_map/psum | solution.py:30
  69.8 159.8 %all-gather.6.cloned.1.call-start = ((), (), s32[]{:S(2)}) async-start(), calls=%async_computation.3 | async-start | bytes 1114112 | tf_op jit(solution)/shard_map/all_gather | solution.py:31
  182.2 188.2 %all-reduce.5.cloned.1.call-start = ((), (), s32[]{:S(2)}) async-start(), calls=%async_computation.2 | async-start | bytes 6291456 | tf_op jit(solution)/shard_map/psum | solution.py:34
  255.3 8.7 %copy-start = (bf16[768,128]{1,0:T(8,128)(2,1)}, bf16[768,128]{1,0:T(8,128)(2,1)S(1)}, u32[]{:S(2)}) copy-start(bf16[768,128]{1,0:T(8,128)(2,1)S(1)} %convolution_convert_fusion) | copy-start | bytes 589828
Sparse Core Ops, SparseCore 0:
  10.5 51.7 all-gather.3
  69.9 109.6 all-reduce.2
  182.9 46.6 all-gather.5
  264.1 106.1 all-reduce.4
